TPU v7x, 256 devices: a whole 4x4x8 slice. The times are simulated.
256 devices in a mesh: dp: 8 (over y, z_lo), owner: 32 (over x, z_hi, core).
Axes of the slice: x: 4, y: 4, z: 8 (z_hi: 4, z_lo: 2; z = z_hi * 2 + z_lo), core: 2. Of those that a mesh axis runs over, the one named last changes fastest.
Arguments:
- partials: bfloat16 [256, 96, 128, 128], P(('dp', 'owner')), may hold values from -1.75 to 1.75
- owners: int32 [96], replicated, may hold values from 0 to 31, as said below
- step_count: int32 [1], replicated, may hold values from 1 to 49
- master: float32 [192, 128, 128], P('owner'), may hold values from -0.3125 to 0.3125
- moment: float32 [192, 128, 128], P('owner'), may hold values from -4 to 4
- second: float32 [192, 128, 128], P('owner'), may hold values from 0.1 to 10
- stat_left: float32 [192, 128, 128], P('owner'), may hold values from -1.5 to 82
- stat_right: float32 [192, 128, 128], P('owner'), may hold values from -1.5 to 82
- basis_left: float32 [192, 128, 128], P('owner'), may hold values from -0.12 to 1.12
- basis_right: float32 [192, 128, 128], P('owner'), may hold values from -0.12 to 1.12
Outputs:
- weights_all: bfloat16 [96, 128, 128], replicated
- direction: float32 [192, 128, 128], P('owner')
- left_new: float32 [192, 128, 128], P('owner')
- right_new: float32 [192, 128, 128], P('owner')
Inputs may be any that keep to these rules, and one draw needn't show every extreme that they name: `owners`: each owner index is named by at least one and at most 6 blocks, and some index by exactly 6.
All inputs are finite; a program needn't handle non-finite values.
Results may differ from a plain program's by a relative error of at most 0.0065.
Values may be sent and summed in bfloat16 or wider, within the bound.
A program may use at most 128 MiB of HBM per device.

v0:
```python
import jax
import jax.numpy as jnp
from jax import lax
from jax.sharding import PartitionSpec as P

NS_ITERS = 6


def product(left, right):
    return jnp.matmul(left, right, precision=lax.Precision.HIGHEST)


def transposed(array):
    return jnp.swapaxes(array, 1, 2)


def refresh(stat, basis):
    power = product(stat, basis)
    magnitude = jnp.sqrt(jnp.sum(power * power, axis=(1, 2), keepdims=True))
    iterate = power / (magnitude + 1e-06)
    for repeat_count in range(NS_ITERS):
        iterate = 1.5 * iterate - 0.5 * product(iterate, product(transposed(iterate), iterate))
    return iterate


def slot_layout(owners, slot_count, total_slot_count):
    block_count = owners.shape[0]
    slot_position = jnp.arange(block_count, dtype=jnp.int32)
    before = (owners[:, None] == owners[None, :]) & (
        slot_position[:, None] > slot_position[None, :]
    )
    rank_in = jnp.sum(before.astype(jnp.int32), axis=1)
    target = owners * slot_count + rank_in
    matches = (target[:, None] == jnp.arange(total_slot_count, dtype=jnp.int32)[None, :]).astype(
        jnp.int32
    )
    source = jnp.sum(matches * slot_position[:, None], axis=0)
    occupied = jnp.sum(matches, axis=0)
    return (target, source, occupied)


def soap_update(
    gradient, occupied, moment, second, stat_left, stat_right, basis_left, basis_right, step_count
):
    elapsed = step_count[0].astype(jnp.float32)
    moment_new = 0.95 * moment + 0.05 * gradient
    rotated = product(transposed(basis_left), product(gradient, basis_right))
    rot_moment = product(transposed(basis_left), product(moment_new, basis_right))
    second_new = 0.95 * second + 0.05 * rotated * rotated
    correction = 1.0 - jnp.power(jnp.float32(0.95), elapsed)
    scaled = rot_moment / correction / (jnp.sqrt(second_new / correction) + 1e-08)
    occupied_mask = (occupied > 0)[:, None, None]
    direction = jnp.where(
        occupied_mask, product(basis_left, product(scaled, transposed(basis_right))), 0.0
    )
    left_stat = 0.95 * stat_left + 0.05 * product(gradient, transposed(gradient))
    right_stat = 0.95 * stat_right + 0.05 * product(transposed(gradient), gradient)
    left_new = jnp.where(occupied_mask, refresh(left_stat, basis_left), basis_left)
    right_new = jnp.where(occupied_mask, refresh(right_stat, basis_right), basis_right)
    return (direction, left_new, right_new)


def body(
    partials,
    owners,
    step_count,
    master,
    moment,
    second,
    stat_left,
    stat_right,
    basis_left,
    basis_right,
):
    owner_count = lax.axis_size("owner")
    slot_count = master.shape[0]
    total_slot_count = slot_count * owner_count
    target, source, occupied = slot_layout(owners, slot_count, total_slot_count)
    first_slot = lax.axis_index("owner") * slot_count
    occupied_mine = lax.dynamic_slice_in_dim(occupied, first_slot, slot_count, 0)
    own_part = partials[0]
    mask_all = (occupied > 0).astype(jnp.float32)[:, None, None]
    placed = jnp.take(own_part, source, axis=0).astype(jnp.float32) * mask_all
    summed = lax.psum_scatter(placed.astype(jnp.bfloat16), "owner", scatter_dimension=0, tiled=True)
    gradient = lax.psum(summed, "dp").astype(jnp.float32)
    direction, left_new, right_new = soap_update(
        gradient,
        occupied_mine,
        moment,
        second,
        stat_left,
        stat_right,
        basis_left,
        basis_right,
        step_count,
    )
    updated = (master - 0.01 * (direction + 0.1 * master)).astype(jnp.bfloat16)
    every_slot = lax.all_gather(updated, "owner", axis=0, tiled=True)
    weights_all = jnp.take(every_slot, target, axis=0)
    return (weights_all, direction, left_new, right_new)


def solution(mesh):
    placed = (
        P(("dp", "owner"), None, None, None),
        P(),
        P(),
        P("owner", None, None),
        P("owner", None, None),
        P("owner", None, None),
        P("owner", None, None),
        P("owner", None, None),
        P("owner", None, None),
        P("owner", None, None),
    )
    return jax.shard_map(
        body,
        mesh=mesh,
        in_specs=placed,
        out_specs=(P(), P("owner", None, None), P("owner", None, None), P("owner", None, None)),
        check_vma=False,
    )
```

profile of v0, /device:TPU:1, one launch (start us, length us, event | category | flops | bytes accessed | tf_op | source)
XLA Modules:
  0.0 320.2 jit_solution(9611837866176556709)
XLA Ops:
  7.2 1.0 convert_reduce_fusion.1
  8.2 0.7 compare_and_fusion.1
  9.1 8.0 %gather_fusion = bf16[192,128,128]{2,1,0:T(8,128)(2,1)} fusion(bf16[96,128,128]{2,1,0:T(8,128)(2,1)S(1)} %bitcast.85, s32[1024]{0:T(1024)S(1)} %pad_clamp_fusion.1), kind=kCustom, calls=%fused_computation | custom fusion | bytes 12583680 | tf_op jit(solution)/shard_map/jit(_take)/gather | solution.py:83
  17.1 8.6 %copy.70 = bf16[192,128,128]{1,2,0:T(8,128)(2,1)} copy(bf16[192,128,128]{2,1,0:T(8,128)(2,1)} %gather_fusion) | data formatting | bytes 12582912 | tf_op jit(solution)/shard_map/jit(_take)/gather | solution.py:83
  25.7 7.5 %multiply_convert_fusion = bf16[192,128,128]{1,2,0:T(8,128)(2,1)} fusion(f32[192]{0:T(256)S(1)} %get-tuple-element.30, bf16[192,128,128]{1,2,0:T(8,128)(2,1)} %copy.70, pred[192]{0:T(512)(128)(4,1)S(1)} %get-tuple-element.31), kind=kLoop, calls=%fused_computation.2 | loop fusion | flops 12582912 | bytes 12583872 | tf_op jit(solution)/shard_map/convert_element_type | solution.py:84
  33.3 112.5 %reduce-scatter.2.cloned.1.call-done = bf16[6,128,128]{1,2,0:T(8,128)(2,1)} async-done(((bf16[192,128,128]{1,2,0:T(8,128)(2,1)}), bf16[6,128,128]{1,2,0:T(8,128)(2,1)}) %reduce-scatter.2.cloned.1.call-update) | async-done | bytes 196624 | tf_op jit(solution)/shard_map/reduce_scatter | solution.py:84
  146.0 1.9 copy.73
  148.5 1.9 copy.69
  150.5 1.9 copy.79
  152.5 67.6 %all-reduce.2.cloned.1.call-done = bf16[6,128,128]{1,2,0:T(8,128)(2,1)} async-done(((bf16[6,128,128]{1,2,0:T(8,128)(2,1)}), bf16[6,128,128]{1,2,0:T(8,128)(2,1)}) %all-reduce.2.cloned.1.call-update) | async-done | bytes 196624 | tf_op jit(solution)/shard_map/psum | solution.py:85
  220.1 1.5 fusion.35
  221.6 1.8 fusion.22
  223.4 1.9 fusion.23
  225.3 1.5 fusion
  227.3 1.8 subtract_convert_fusion
  229.1 1.7 copy.80
  230.9 1.9 copy.92
  232.8 1.9 copy.81
  234.7 1.9 copy.102
  236.6 1.5 fusion.2
  238.1 0.9 multiply_reduce_fusion
  239.0 1.5 fusion.1
  240.5 1.9 multiply_reduce_fusion.1
  242.4 0.9 fusion.31
  243.3 0.9 fusion.30
  244.2 0.6 fusion.9
  244.8 0.8 fusion.42
  245.6 0.6 fusion.8
  246.2 0.8 fusion.43
  247.0 0.6 fusion.7
  247.6 1.0 fusion.44
  249.2 0.8 fusion.45
  250.0 0.6 fusion.5
  250.5 0.8 fusion.46
  251.4 0.6 fusion.16
  252.0 0.8 fusion.37
  252.8 0.6 fusion.15
  253.4 0.8 fusion.38
  254.8 0.8 fusion.39
  255.6 0.6 fusion.13
  256.1 0.8 fusion.40
  257.0 0.6 fusion.12
  257.5 0.8 fusion.41
  258.3 1.3 fusion.4
  259.7 1.3 fusion.11
  261.0 43.3 %all-gather.2.cloned.1.call-done = bf16[192,128,128]{2,1,0:T(8,128)(2,1)} async-done(((bf16[6,128,128]{2,1,0:T(8,128)(2,1)}), bf16[192,128,128]{2,1,0:T(8,128)(2,1)}) %all-gather.2.cloned.1.call-update) | async-done | bytes 6291472 | tf_op jit(solution)/shard_map/all_gather | solution.py:98
  304.3 5.5 %gather_fusion.1 = bf16[96,128,128]{2,1,0:T(8,128)(2,1)} fusion(bf16[192,128,128]{2,1,0:T(8,128)(2,1)} %all-gather.2.cloned.1.call-done, s32[1024]{0:T(1024)S(1)} %pad_clamp_fusion), kind=kCustom, calls=%fused_computation.1 | custom fusion | bytes 6291840 | tf_op jit(solution)/shard_map/jit(_take)/gather | solution.py:99
  309.8 3.9 %broadcast_select_fusion = bf16[96,128,128]{2,1,0:T(8,128)(2,1)} fusion(bf16[96,128,128]{2,1,0:T(8,128)(2,1)} %gather_fusion.1, pred[96]{0:T(512)(128)(4,1)S(1)} %get-tuple-element.22), kind=kLoop, calls=%fused_computation.3 | loop fusion | flops 1572864 | bytes 6291552 | tf_op jit(solution)/shard_map/jit(_take)/select_n | solution.py:99
  (28 shorter events, 2.2 us)
Async XLA Ops:
  7.2 1.9 copy-start
  7.2 138.6 %reduce-scatter.2.cloned.1.call-start = ((), (), s32[]{:S(2)}) async-start(), calls=%async_computation.1 | async-start | bytes 6488064 | tf_op jit(solution)/shard_map/reduce_scatter | solution.py:84
  33.2 186.9 %copy-start.1 = (f32[6,128,128]{2,1,0:T(8,128)S(1)}, f32[6,128,128]{2,1,0:T(8,128)}, u32[]{:S(2)}) copy-start(f32[6,128,128]{2,1,0:T(8,128)} %param.19) | copy-start | bytes 1179652
  33.2 186.8 %all-reduce.2.cloned.1.call-start = ((), (), s32[]{:S(2)}) async-start(), calls=%async_computation.2 | async-start | bytes 393216 | tf_op jit(solution)/shard_map/psum | solution.py:85
  145.8 158.6 %all-gather.2.cloned.1.call-start = ((), (), s32[]{:S(2)}) async-start(), calls=%async_computation.3 | async-start | bytes 6488064 | tf_op jit(solution)/shard_map/all_gather | solution.py:98
  220.1 7.2 %copy-start.2 = (f32[6,128,128]{2,1,0:T(8,128)S(1)}, f32[6,128,128]{2,1,0:T(8,128)}, u32[]{:S(2)}) copy-start(f32[6,128,128]{2,1,0:T(8,128)} %param.18) | copy-start | bytes 1179652
  220.1 7.2 %copy-start.4 = (f32[6,128,128]{1,2,0:T(8,128)S(1)}, f32[6,128,128]{1,2,0:T(8,128)}, u32[]{:S(2)}) copy-start(f32[6,128,128]{1,2,0:T(8,128)} %copy.79) | copy-start | bytes 1179652
  252.0 7.7 %copy-start.3 = (f32[6,128,128]{2,1,0:T(8,128)S(1)}, f32[6,128,128]{2,1,0:T(8,128)}, u32[]{:S(2)}) copy-start(f32[6,128,128]{2,1,0:T(8,128)} %param.18) | copy-start | bytes 1179652
Sparse Core Ops, SparseCore 0:
  33.3 112.3 reduce-scatter.1
  148.5 71.5 all-reduce.1
  231.0 73.2 all-gather.1
where the time goes:
time: 321 us; the launch traced here: 320 us
  waiting for transfers between devices  223 us (69%)
  local copies, waits for them, and re-layouts  35.4 us (11%)
  matrix products  33.2 us (10%)
  between operations  14.7 us (5%)
  other arithmetic  13.3 us (4%)
    reduce_scatter x1, waiting for transfers between devices, body(): lax.psum_scatter(placed.astype(jnp.bfloat16), 'owner', scatter_dimension=...  112 us
    psum x1, waiting for transfers between devices, body(): gradient = lax.psum(summed, 'dp').astype(jnp.float32)  67.6 us
    all_gather x1, waiting for transfers between devices, body(): every_slot = lax.all_gather(updated, 'owner', axis=0, tiled=True)  43.3 us
    dot_general x34, matrix products, product(): return jnp.matmul(left, right, precision=lax.Precision.HIGHEST)  33.2 us
    gather x2, local copies, waits for them, and re-layouts, body(): placed = jnp.take(own_part, source, axis=0).astype(jnp.float32) * mask_all  16.6 us
    unnamed x16, local copies, waits for them, and re-layouts  11.5 us
    convert_element_type x1, other arithmetic, body(): placed.astype(jnp.bfloat16)  7.46 us
  transfers between devices with their start and end apart: 3, of which 3 were waited for; matrix products, arithmetic and copies ran while one was open for 11% of the time, Pallas kernels for 0%

commit v1 on v0

--- a/solution.py
+++ b/solution.py
@@ -82,7 +82,7 @@
     mask_all = (occupied > 0).astype(jnp.float32)[:, None, None]
     placed = jnp.take(own_part, source, axis=0).astype(jnp.float32) * mask_all
     summed = lax.psum_scatter(placed.astype(jnp.bfloat16), "owner", scatter_dimension=0, tiled=True)
-    gradient = lax.psum(summed, "dp").astype(jnp.float32)
+    gradient = jnp.sum(lax.all_gather(summed, "dp"), axis=0).astype(jnp.float32)
     direction, left_new, right_new = soap_update(
         gradient,
         occupied_mine,

time: 321 us -> 284 us (0.88)
  waiting for transfers between devices: 223 us -> 190 us
  local copies, waits for them, and re-layouts: 35.4 us -> 28.5 us
    psum x1 -> x0, waiting for transfers between devices: 67.6 us -> none  [body(): gradient = lax.psum(summed, 'dp').astype(jnp.float32)]
    all_gather x0 -> x1, waiting for transfers between devices: none -> 37.6 us  [body(): gradient = jnp.sum(lax.all_gather(summed, 'dp'), axis=0).astype(jnp.float32)]
    gather x2 -> x1, local copies, waits for them, and re-layouts: 16.6 us -> 8.01 us  [body(): placed = jnp.take(own_part, source, axis=0).astype(jnp.float32) * mask_all]
  transfers between devices with their start and end apart: 3 -> 3, of which waited for: 3 -> 3; matrix products, arithmetic and copies ran while one was open for 11% -> 13% of each run, Pallas kernels for 0% -> 0%
where the time goes in v1:
time: 284 us; the launch traced here: 283 us
  waiting for transfers between devices  190 us (67%)
  matrix products  33 us (12%)
  local copies, waits for them, and re-layouts  28.5 us (10%)
  other arithmetic  15.7 us (6%)
  between operations  14.9 us (5%)
    reduce_scatter x1, waiting for transfers between devices, body(): lax.psum_scatter(placed.astype(jnp.bfloat16), 'owner', scatter_dimension=...  112 us
    all_gather x1, waiting for transfers between devices, body(): every_slot = lax.all_gather(updated, 'owner', axis=0, tiled=True)  40.4 us
    all_gather x1, waiting for transfers between devices, body(): gradient = jnp.sum(lax.all_gather(summed, 'dp'), axis=0).astype(jnp.float32)  37.6 us
    dot_general x34, matrix products, product(): return jnp.matmul(left, right, precision=lax.Precision.HIGHEST)  33 us
    unnamed x16, local copies, waits for them, and re-layouts  11.5 us
    gather x1, local copies, waits for them, and re-layouts, body(): placed = jnp.take(own_part, source, axis=0).astype(jnp.float32) * mask_all  8.01 us
    convert_element_type x1, other arithmetic, body(): placed.astype(jnp.bfloat16)  7.5 us
  transfers between devices with their start and end apart: 3, of which 3 were waited for; matrix products, arithmetic and copies ran while one was open for 13% of the time, Pallas kernels for 0%

profile of v1, /device:TPU:1, one launch (start us, length us, event | category | flops | bytes accessed | tf_op | source)
XLA Modules:
  0.0 282.8 jit_solution(10120646255417960455)
XLA Ops:
  7.2 1.0 convert_reduce_fusion.1
  8.2 0.7 compare_and_fusion.1
  9.1 8.0 %gather_fusion = bf16[192,128,128]{2,1,0:T(8,128)(2,1)} fusion(bf16[96,128,128]{2,1,0:T(8,128)(2,1)S(1)} %bitcast.86, s32[1024]{0:T(1024)S(1)} %pad_clamp_fusion.1), kind=kCustom, calls=%fused_computation | custom fusion | bytes 12583680 | tf_op jit(solution)/shard_map/jit(_take)/gather | solution.py:83
  17.1 7.5 %multiply_convert_fusion = bf16[192,128,128]{2,1,0:T(8,128)(2,1)} fusion(f32[192]{0:T(256)S(1)} %get-tuple-element.30, bf16[192,128,128]{2,1,0:T(8,128)(2,1)} %gather_fusion, pred[192]{0:T(512)(128)(4,1)S(1)} %get-tuple-element.31), kind=kLoop, calls=%fused_computation.2 | loop fusion | flops 12582912 | bytes 12583872 | tf_op jit(solution)/shard_map/convert_element_type | solution.py:84
  24.7 112.4 %reduce-scatter.2.cloned.1.call-done = bf16[6,128,128]{2,1,0:T(8,128)(2,1)} async-done(((bf16[192,128,128]{2,1,0:T(8,128)(2,1)}), bf16[6,128,128]{2,1,0:T(8,128)(2,1)}) %reduce-scatter.2.cloned.1.call-update) | async-done | bytes 196624 | tf_op jit(solution)/shard_map/reduce_scatter | solution.py:84
  137.3 1.9 copy.74
  139.2 1.9 copy.69
  141.8 1.9 copy.65
  143.8 37.6 %all-gather.6.cloned.1.call-done = bf16[48,128,128]{2,1,0:T(8,128)(2,1)} async-done(((bf16[6,128,128]{2,1,0:T(8,128)(2,1)}), bf16[48,128,128]{2,1,0:T(8,128)(2,1)}) %all-gather.6.cloned.1.call-update) | async-done | bytes 1572880 | tf_op jit(solution)/shard_map/all_gather | solution.py:85
  181.4 2.4 reduce_sum.63
  183.8 1.7 copy.66
  185.5 1.5 fusion.35
  187.0 1.9 fusion.23
  188.9 1.8 fusion.22
  190.7 1.5 fusion
  192.8 1.8 subtract_convert_fusion
  194.6 1.7 copy.75
  196.3 1.9 copy.76
  198.2 1.9 copy.85
  200.2 1.9 copy.95
  202.1 1.5 fusion.1
  203.5 1.9 multiply_reduce_fusion.1
  205.4 1.5 fusion.2
  206.9 0.9 multiply_reduce_fusion
  207.8 0.9 fusion.30
  208.7 0.9 fusion.31
  209.6 0.6 fusion.16
  210.2 0.8 fusion.37
  211.1 0.6 fusion.15
  211.6 0.8 fusion.38
  212.5 0.6 fusion.14
  213.2 0.8 fusion.39
  214.6 0.8 fusion.40
  215.4 0.6 fusion.12
  216.0 0.8 fusion.41
  216.8 0.6 fusion.9
  217.5 0.8 fusion.42
  218.3 0.6 fusion.8
  218.8 0.8 fusion.43
  220.2 0.8 fusion.44
  221.0 0.6 fusion.6
  221.6 0.8 fusion.45
  223.0 0.8 fusion.46
  223.8 1.3 fusion.11
  225.2 1.3 fusion.4
  226.5 40.4 %all-gather.4.cloned.1.call-done = bf16[192,128,128]{2,1,0:T(8,128)(2,1)} async-done(((bf16[6,128,128]{2,1,0:T(8,128)(2,1)}), bf16[192,128,128]{2,1,0:T(8,128)(2,1)}) %all-gather.4.cloned.1.call-update) | async-done | bytes 6291472 | tf_op jit(solution)/shard_map/all_gather | solution.py:98
  266.9 5.5 %gather_fusion.1 = bf16[96,128,128]{2,1,0:T(8,128)(2,1)} fusion(bf16[192,128,128]{2,1,0:T(8,128)(2,1)} %all-gather.4.cloned.1.call-done, s32[1024]{0:T(1024)S(1)} %pad_clamp_fusion), kind=kCustom, calls=%fused_computation.1 | custom fusion | bytes 6291840 | tf_op jit(solution)/shard_map/jit(_take)/gather | solution.py:99
  272.4 3.9 %broadcast_select_fusion = bf16[96,128,128]{2,1,0:T(8,128)(2,1)} fusion(bf16[96,128,128]{2,1,0:T(8,128)(2,1)} %gather_fusion.1, pred[96]{0:T(512)(128)(4,1)S(1)} %get-tuple-element.22), kind=kLoop, calls=%fused_computation.3 | loop fusion | flops 1572864 | bytes 6291552 | tf_op jit(solution)/shard_map/jit(_take)/select_n | solution.py:99
  (29 shorter events, 2.8 us)
Async XLA Ops:
  7.2 1.9 copy-start
  7.2 129.9 %reduce-scatter.2.cloned.1.call-start = ((), (), s32[]{:S(2)}) async-start(), calls=%async_computation.1 | async-start | bytes 6488064 | tf_op jit(solution)/shard_map/reduce_scatter | solution.py:84
  24.6 160.9 %copy-start.1 = (f32[6,128,128]{2,1,0:T(8,128)S(1)}, f32[6,128,128]{2,1,0:T(8,128)}, u32[]{:S(2)}) copy-start(f32[6,128,128]{2,1,0:T(8,128)} %param.19) | copy-start | bytes 1179652
  24.6 156.8 %all-gather.6.cloned.1.call-start = ((), (), s32[]{:S(2)}) async-start(), calls=%async_computation.3 | async-start | bytes 1769472 | tf_op jit(solution)/shard_map/all_gather | solution.py:85
  137.1 129.8 %all-gather.4.cloned.1.call-start = ((), (), s32[]{:S(2)}) async-start(), calls=%async_computation.2 | async-start | bytes 6488064 | tf_op jit(solution)/shard_map/all_gather | solution.py:98
  185.5 7.2 %copy-start.2 = (f32[6,128,128]{2,1,0:T(8,128)S(1)}, f32[6,128,128]{2,1,0:T(8,128)}, u32[]{:S(2)}) copy-start(f32[6,128,128]{2,1,0:T(8,128)} %param.18) | copy-start | bytes 1179652
  185.5 7.2 %copy-start.4 = (f32[6,128,128]{1,2,0:T(8,128)S(1)}, f32[6,128,128]{1,2,0:T(8,128)}, u32[]{:S(2)}) copy-start(f32[6,128,128]{1,2,0:T(8,128)} %copy.74) | copy-start | bytes 1179652
  216.8 7.0 %copy-start.3 = (f32[6,128,128]{2,1,0:T(8,128)S(1)}, f32[6,128,128]{2,1,0:T(8,128)}, u32[]{:S(2)}) copy-start(f32[6,128,128]{2,1,0:T(8,128)} %param.18) | copy-start | bytes 1179652
Sparse Core Ops, SparseCore 0:
  24.8 112.2 reduce-scatter.1
  139.0 42.3 all-gather.5
  196.4 70.3 all-gather.3
